TPU v7x, 32 devices: a whole 2x2x4 slice. The times are simulated.
32 devices in a mesh: group: 4 (over y, core), tile: 8 (over z, x).
Axes of the slice: x: 2, y: 2, z: 4, core: 2. Of those that a mesh axis runs over, the one named last changes fastest.
Arguments:
- checkpoint: float32 [16, 512, 768], P(None, ('group', 'tile')), may hold values from -6 to 6
- adjoint_in: float32 [16, 512, 768], P(None, ('group', 'tile')), may hold values from -6 to 6
- courant_x: float32 [16, 512, 768], P(None, ('group', 'tile')), may hold values from 0.05 to 0.5
- courant_y: float32 [16, 512, 768], P(None, ('group', 'tile')), may hold values from 0.05 to 0.5
- mixing: float32 [15, 512, 768], P(None, ('group', 'tile')), may hold values from 0.02 to 0.3
- snd_column: int32 [32, 8, 128], P(('group', 'tile')), may hold values from 0 to 12287
- snd_count: int32 [32, 8], P(('group', 'tile')), may hold values from 32 to 128, as said below
- snd_step: int32 [32, 8, 128], P(('group', 'tile')), may hold values from 0 to 1
- snd_value: float32 [32, 8, 128], P(('group', 'tile')), may hold values from -6 to 6
- snd_weight: float32 [32, 8, 128], P(('group', 'tile')), may hold values from 0.3 to 3
- snd_kernel: float32 [32, 8, 16, 128], P(('group', 'tile')), may hold values from 0 to 0.5
Outputs:
- adjoint_out: float32 [16, 512, 768], P(None, ('group', 'tile'))
Inputs may be any that keep to these rules, and one draw needn't show every extreme that they name: `snd_count`: at most 128; in every draw some destination tile receives 128 soundings from every source device of each group, and every source device fills all slots of some destination tile.
All inputs are finite; a program needn't handle non-finite values.
Results may differ from a plain program's by a relative error of at most 0.0001.
Values sent between devices are 32-bit elements; how exact they have to be, the bound alone decides.
A program may use at most 64 MiB of HBM per device.

v0:
```python
import jax
import jax.numpy as jnp
from jax import lax
from jax.sharding import PartitionSpec as P

STEPS = 2


def with_halo(block, sides, width):
    for axis, dim in sides:
        count = lax.axis_size(axis)
        forward = [(i, i + 1) for i in range(count - 1)]
        forward.append((count - 1, 0))
        backward = [(target, source) for source, target in forward]
        low = lax.ppermute(
            lax.slice_in_dim(block, block.shape[dim] - width, None, axis=dim), axis, forward
        )
        high = lax.ppermute(lax.slice_in_dim(block, 0, width, axis=dim), axis, backward)
        block = jnp.concatenate([low, block, high], axis=dim)
    return block


def from_behind(block, axis, distance):
    devices = range(lax.axis_size(axis))
    route = [((i - distance) % len(devices), i) for i in devices]
    return lax.ppermute(block, axis, route)


def pad_periodic(field, width, along):
    total = field.shape[along]
    return jnp.concatenate(
        [
            lax.slice_in_dim(field, total - width, total, axis=along),
            field,
            lax.slice_in_dim(field, 0, width, axis=along),
        ],
        axis=along,
    )


def sweep_forward(padded, courant_pad, along):
    interior = padded.shape[along] - 4

    def piece_of(first, last):
        return lax.slice_in_dim(padded, first, last, axis=along)

    courant_face = lax.slice_in_dim(courant_pad, 0, interior + 1, axis=along)
    fluxes = (
        courant_face
        * (
            2.0 * piece_of(2, interior + 3)
            + 5.0 * piece_of(1, interior + 2)
            - piece_of(0, interior + 1)
        )
        / 6.0
    )
    return (
        piece_of(2, interior + 2)
        + lax.slice_in_dim(fluxes, 0, interior, axis=along)
        - lax.slice_in_dim(fluxes, 1, interior + 1, axis=along)
    )


def sweep_adjoint(padded, courant_pad, along):
    interior = padded.shape[along] - 4

    def piece_of(first, last):
        return lax.slice_in_dim(padded, first, last, axis=along)

    differences = piece_of(2, interior + 4) - piece_of(1, interior + 3)
    scaled = courant_pad * differences
    return (
        piece_of(2, interior + 2)
        + (
            2.0 * lax.slice_in_dim(scaled, 0, interior, axis=along)
            + 5.0 * lax.slice_in_dim(scaled, 1, interior + 1, axis=along)
            - lax.slice_in_dim(scaled, 2, interior + 2, axis=along)
        )
        / 6.0
    )


def vertical_mix(field, mixing):
    fluxes = mixing * (field[1:] - field[:-1])
    zero_row = jnp.zeros_like(field[:1])
    return (
        field
        + jnp.concatenate([fluxes, zero_row], axis=0)
        - jnp.concatenate([zero_row, fluxes], axis=0)
    )


def horizontal(rimmed, wind_x, wind_y):
    swept = sweep_forward(rimmed, wind_x, 1)
    return sweep_forward(pad_periodic(swept, 2, 2), wind_y, 2)


def on_device(
    checkpoint,
    adjoint_in,
    courant_x,
    courant_y,
    mixing,
    snd_column,
    snd_count,
    snd_step,
    snd_value,
    snd_weight,
    snd_kernel,
):
    levels, width_x, width_y = checkpoint.shape
    tile_count = snd_column.shape[1]
    capacity = snd_column.shape[2]
    wind_x = with_halo(courant_x, ((("group", "tile"), 1),), 1)
    wind_y = pad_periodic(courant_y, 1, 2)
    tracer = from_behind(checkpoint, "group", 1)
    rimmed = with_halo(tracer, ((("group", "tile"), 1),), 2)
    tracer = vertical_mix(horizontal(rimmed, wind_x, wind_y), mixing)
    states = [tracer]
    moment = 1
    rimmed = with_halo(tracer, ((("group", "tile"), 1),), 2)
    tracer = vertical_mix(horizontal(rimmed, wind_x, wind_y), mixing)
    states.append(tracer)
    position = lax.broadcasted_iota(jnp.int32, snd_column.shape, 2)
    weight = jnp.where(position < snd_count[:, :, None], snd_weight, jnp.zeros_like(snd_weight))
    values, weights, kernels = (
        lax.all_to_all(snd_value, "tile", split_axis=1, concat_axis=0, tiled=True),
        lax.all_to_all(weight, "tile", split_axis=1, concat_axis=0, tiled=True),
        lax.all_to_all(snd_kernel, "tile", split_axis=1, concat_axis=0, tiled=True),
    )
    columns, step_ids = (
        lax.all_to_all(snd_column, "tile", split_axis=1, concat_axis=0, tiled=True),
        lax.all_to_all(snd_step, "tile", split_axis=1, concat_axis=0, tiled=True),
    )
    values = values.reshape(tile_count, capacity)
    weights = weights.reshape(tile_count, capacity)
    kernels = kernels.reshape(tile_count, levels, capacity)
    step_ids = step_ids.reshape(tile_count, capacity)
    cell_index = columns.reshape(-1)
    forcings = []
    for moment in range(STEPS):
        flattened = states[moment].reshape(levels, -1)
        picked = jnp.take(flattened, cell_index, axis=1).reshape(levels, tile_count, capacity)
        observed = jnp.einsum("ltc,tlc->tc", picked, kernels, precision=lax.Precision.HIGHEST)
        misfit = jnp.where(
            step_ids == moment, weights * (observed - values), jnp.zeros_like(observed)
        )
        contribution = jnp.einsum(
            "tlc,tc->ltc", kernels, misfit, precision=lax.Precision.HIGHEST
        ).reshape(levels, -1)
        forcing = (
            jnp.zeros((levels, width_x * width_y), jnp.float32).at[:, cell_index].add(contribution)
        )
        forcings.append(forcing.reshape(levels, width_x, width_y))
    adjoint = adjoint_in
    for moment in reversed(range(STEPS)):
        adjoint = vertical_mix(adjoint + forcings[moment], mixing)
        adjoint = sweep_adjoint(pad_periodic(adjoint, 2, 2), wind_y, 2)
        rimmed = with_halo(adjoint, ((("group", "tile"), 1),), 2)
        adjoint = sweep_adjoint(rimmed, wind_x, 1)
    return adjoint


def solution(mesh):
    return jax.shard_map(
        on_device,
        mesh=mesh,
        in_specs=(
            P(None, ("group", "tile"), None),
            P(None, ("group", "tile"), None),
            P(None, ("group", "tile"), None),
            P(None, ("group", "tile"), None),
            P(None, ("group", "tile"), None),
            P(("group", "tile"), None, None),
            P(("group", "tile"), None),
            P(("group", "tile"), None, None),
            P(("group", "tile"), None, None),
            P(("group", "tile"), None, None),
            P(("group", "tile"), None, None, None),
        ),
        out_specs=P(None, ("group", "tile"), None),
        check_vma=False,
    )
```

profile of v0, /device:TPU:0, one launch (start us, length us, event | category | flops | bytes accessed | tf_op | source)
XLA Modules:
  0.0 144.3 jit_solution(1064985473383274465)
XLA Ops:
  0.0 7.4 %all-to-all-start = ((s32[1,8,128]{2,0,1:T(1,128)}), s32[1,8,128]{2,0,1:T(1,128)S(1)}, u32[]{:S(2)}, u32[]{:S(2)}) async-start(s32[1,8,128]{2,0,1:T(1,128)} %bitcast.75), calls=%async_computation | async-start | bytes 8192 | tf_op jit(solution)/shard_map/all_to_all | solution.py:132
  7.4 1.8 %fusion.56 = (f32[16,1,768]{2,1,0:T(1,128)}, f32[16,1,768]{2,1,0:T(1,128)S(1)}) fusion(f32[16,16,768]{2,1,0:T(8,128)} %param.15), kind=kLoop, calls=%fused_computation.126 | loop fusion | bytes 196608 | tf_op jit(solution)/shard_map/slice | solution.py:18
  9.2 2.0 %collective-permute-start.1 = (f32[16,1,768]{2,1,0:T(1,128)S(1)}, f32[16,1,768]{2,1,0:T(1,128)S(1)}, u32[]{:S(2)}, u32[]{:S(2)}) collective-permute-start(f32[16,1,768]{2,1,0:T(1,128)S(1)} %get-tuple-element.13), channel_id=1, source_target_pairs={{0,1},{1,2},{2,3},{3,4},{4,5},{5,6},{6,7},{7,8},{8,9},{9,10},{10,1... | collective-permute-start | bytes 147464 | tf_op jit(solution)/shard_map/ppermute | solution.py:15
  11.2 1.1 fusion.58
  12.3 1.4 compare_select_fusion.1
  13.8 5.0 %all-to-all-start.2 = ((f32[1,8,128]{2,0,1:T(1,128)}), f32[1,8,128]{2,0,1:T(1,128)S(1)}, u32[]{:S(2)}, u32[]{:S(2)}) async-start(f32[1,8,128]{2,0,1:T(1,128)} %compare_select_fusion.1), calls=%async_computation.2 | async-start | bytes 8192 | tf_op jit(solution)/shard_map/all_to_all | solution.py:128
  18.9 0.7 collective-permute-done
  19.6 1.6 %collective-permute-start.3 = (f32[16,2,768]{2,1,0:T(2,128)S(1)}, f32[16,2,768]{2,1,0:T(2,128)S(1)}, u32[]{:S(2)}, u32[]{:S(2)}) collective-permute-start(f32[16,2,768]{2,1,0:T(2,128)S(1)} %get-tuple-element.27), channel_id=1, source_target_pairs={{0,1},{1,2},{2,3},{3,4},{4,5},{5,6},{6,7},{7,8},{8,9},{9,10},{10,1... | collective-permute-start | bytes 294920 | tf_op jit(solution)/shard_map/ppermute | solution.py:15
  21.2 3.8 %collective-permute-start.2 = (f32[16,2,768]{2,1,0:T(2,128)S(1)}, f32[16,2,768]{2,1,0:T(2,128)S(1)}, u32[]{:S(2)}, u32[]{:S(2)}) collective-permute-start(f32[16,2,768]{2,1,0:T(2,128)S(1)} %get-tuple-element.26), channel_id=1, source_target_pairs={{1,0},{2,1},{3,2},{4,3},{5,4},{6,5},{7,6},{8,7},{9,8},{10,9},{11,1... | collective-permute-start | bytes 294920 | tf_op jit(solution)/shard_map/ppermute | solution.py:18
  25.1 3.3 %collective-permute-done.3 = f32[16,2,768]{2,1,0:T(2,128)S(1)} collective-permute-done((f32[16,2,768]{2,1,0:T(2,128)S(1)}, f32[16,2,768]{2,1,0:T(2,128)S(1)}, u32[]{:S(2)}, u32[]{:S(2)}) %collective-permute-start.3) | collective-permute-done | bytes 98336 | tf_op jit(solution)/shard_map/ppermute | solution.py:15
  28.4 0.6 fusion.15
  29.2 0.9 copy-done
  30.1 0.8 fusion.29
  31.3 0.8 copy-done.2
  32.2 0.7 fusion.61
  33.0 5.3 %collective-permute-start.4 = (f32[16,2,768]{2,1,0:T(2,128)}, f32[16,2,768]{2,1,0:T(2,128)}, u32[]{:S(2)}, u32[]{:S(2)}) collective-permute-start(f32[16,2,768]{2,1,0:T(2,128)} %get-tuple-element.22), channel_id=1, source_target_pairs={{1,0},{2,1},{3,2},{4,3},{5,4},{6,5},{7,6},{8,7},{9,8},{10,9},{11,1... | collective-permute-start | bytes 294920 | tf_op jit(solution)/shard_map/ppermute | solution.py:18
  38.3 3.9 %copy.49 = f32[16,16,768]{0,2,1:T(8,128)} copy(f32[16,16,768]{2,1,0:T(8,128)S(1)} %pad_subtract_fusion.3) | data formatting | bytes 1572864 | tf_op jit(solution)/shard_map/sub | solution.py:87
  42.3 6.8 %gather_fusion.1 = f32[1024,16]{1,0:T(8,128)} fusion(f32[16,12288]{0,1:T(8,128)} %bitcast.66, s32[1024]{0:T(1024)S(1)} %fusion.53), kind=kCustom, calls=%fused_computation.1.clone | custom fusion | bytes 135168 | tf_op jit(solution)/shard_map/jit(_take)/gather | solution.py:143
  49.1 1.5 %fusion.10 = f32[16,17,768]{2,1,0:T(8,128)S(1)} fusion(f32[16,16,768]{2,1,0:T(8,128)S(1)} %pad_subtract_fusion.3, f32[16,2,768]{2,1,0:T(2,128)S(1)} %collective-permute-done.5, f32[16,2,768]{2,1,0:T(2,128)} %collective-permute-done.4, f32[16,16,768]{2,1,0:T(8,128)S(1)} %copy-done.1, f32[16,1,768]{2,1,0:T(1,128)S(1)} %collective-permute-done.1), kind=kLoop, calls=%fused_computation.19 | loop fusion | flops 2088960 | bytes 2654208 | tf_op jit(solution)/shard_map/div | solution.py:49
  50.8 0.8 fusion.24
  52.0 0.9 fusion.47
  52.9 3.3 %all-to-all-start.4 = ((f32[1,8,128]{2,0,1:T(1,128)}), f32[1,8,128]{2,0,1:T(1,128)S(1)}, u32[]{:S(2)}, u32[]{:S(2)}) async-start(f32[1,8,128]{2,0,1:T(1,128)} %bitcast.22), calls=%async_computation.4 | async-start | bytes 8192 | tf_op jit(solution)/shard_map/all_to_all | solution.py:127
  56.3 2.3 %pad_subtract_fusion.2 = f32[16,16,768]{2,1,0:T(8,128)} fusion(f32[15,16,768]{2,1,0:T(8,128)} %fusion.47, f32[16,16,768]{2,1,0:T(8,128)S(1)} %slice_subtract_fusion.4), kind=kLoop, calls=%fused_computation.95 | loop fusion | flops 393216 | bytes 2310144 | tf_op jit(solution)/shard_map/sub | solution.py:87
  58.6 4.8 %copy.42 = f32[16,16,768]{0,2,1:T(8,128)} copy(f32[16,16,768]{2,1,0:T(8,128)} %pad_subtract_fusion.2) | data formatting | bytes 1572864 | tf_op jit(solution)/shard_map/sub | solution.py:87
  63.5 6.8 %gather_fusion = f32[1024,16]{1,0:T(8,128)} fusion(f32[16,12288]{0,1:T(8,128)} %bitcast.65, s32[1024]{0:T(1024)S(1)} %fusion.53), kind=kCustom, calls=%fused_computation.clone | custom fusion | bytes 135168 | tf_op jit(solution)/shard_map/jit(_take)/gather | solution.py:143
  70.3 5.9 %all-to-all-start.3 = ((f32[1,8,16,128]{3,2,0,1:T(8,128)}), f32[1,8,16,128]{3,2,0,1:T(8,128)S(1)}, u32[]{:S(2)}, u32[]{:S(2)}) async-start(f32[1,8,16,128]{3,2,0,1:T(8,128)} %bitcast.19), calls=%async_computation.3 | async-start | bytes 131072 | tf_op jit(solution)/shard_map/all_to_all | solution.py:129
  76.2 2.2 %broadcast_select_fusion = (f32[1024,16]{1,0:T(8,128)S(1)}, f32[1024,16]{1,0:T(8,128)}) fusion(f32[1024,16]{1,0:T(8,128)} %gather_fusion.1, pred[1024]{0:T(1024)(128)(4,1)S(1)} %compare_and_fusion, f32[1024,16]{1,0:T(8,128)} %gather_fusion), kind=kLoop, calls=%fused_computation.105 | loop fusion | flops 32768 | bytes 263168 | tf_op jit(solution)/shard_map/jit(_take)/select_n | solution.py:143
  78.4 1.2 copy.58
  79.8 3.3 %all-to-all-done.3 = f32[1,8,16,128]{3,2,0,1:T(8,128)S(1)} async-done(((f32[1,8,16,128]{3,2,0,1:T(8,128)}), f32[1,8,16,128]{3,2,0,1:T(8,128)S(1)}, u32[]{:S(2)}, u32[]{:S(2)}) %all-to-all-start.3) | async-done | bytes 65568 | tf_op jit(solution)/shard_map/all_to_all | solution.py:129
  83.1 3.3 %all-to-all-start.1 = ((s32[1,8,128]{2,0,1:T(1,128)}), s32[1,8,128]{2,0,1:T(1,128)S(1)}, u32[]{:S(2)}, u32[]{:S(2)}) async-start(s32[1,8,128]{2,0,1:T(1,128)} %bitcast.7), calls=%async_computation.1 | async-start | bytes 8192 | tf_op jit(solution)/shard_map/all_to_all | solution.py:133
  86.5 6.3 %all-to-all-done.1 = s32[1,8,128]{2,0,1:T(1,128)S(1)} async-done(((s32[1,8,128]{2,0,1:T(1,128)}), s32[1,8,128]{2,0,1:T(1,128)S(1)}, u32[]{:S(2)}, u32[]{:S(2)}) %all-to-all-start.1) | async-done | bytes 4128 | tf_op jit(solution)/shard_map/all_to_all | solution.py:133
  93.0 9.0 %scatter_custom_fusion = f32[16,12288]{0,1:T(8,128)} fusion(s32[1024]{0:T(1024)S(1)} %bitcast.76, f32[1024,16]{1,0:T(8,128)S(1)} %copy.46, f32[]{:T(128)} %constant.15.clone.1), kind=kCustom, calls=%fused_computation.6 | custom fusion | flops 16384 | bytes 786436 | tf_op jit(solution)/shard_map/scatter-add | solution.py:152
  102.1 4.5 %copy.47 = f32[16,16,768]{2,1,0:T(8,128)S(1)} copy(f32[16,16,768]{0,2,1:T(8,128)} %bitcast.64) | data formatting | bytes 1572864 | tf_op jit(solution)/shard_map/reshape | solution.py:154
  106.5 1.2 add.114
  108.0 0.6 fusion.21
  109.2 0.8 fusion.57
  109.9 2.0 %collective-permute-start.8 = (f32[16,2,768]{2,1,0:T(2,128)}, f32[16,2,768]{2,1,0:T(2,128)}, u32[]{:S(2)}, u32[]{:S(2)}) collective-permute-start(f32[16,2,768]{2,1,0:T(2,128)} %get-tuple-element.14), channel_id=1, source_target_pairs={{0,1},{1,2},{2,3},{3,4},{4,5},{5,6},{6,7},{7,8},{8,9},{9,10},{10,1... | collective-permute-start | bytes 294920 | tf_op jit(solution)/shard_map/ppermute | solution.py:15
  111.9 3.3 %collective-permute-start.6 = (f32[16,1,768]{2,1,0:T(1,128)}, f32[16,1,768]{2,1,0:T(1,128)S(1)}, u32[]{:S(2)}, u32[]{:S(2)}) collective-permute-start(f32[16,1,768]{2,1,0:T(1,128)} %get-tuple-element.12), channel_id=1, source_target_pairs={{1,0},{2,1},{3,2},{4,3},{5,4},{6,5},{7,6},{8,7},{9,8},{10,9},{11,1... | collective-permute-start | bytes 147464 | tf_op jit(solution)/shard_map/ppermute | solution.py:18
  115.3 1.0 copy.51
  116.3 9.4 %scatter_custom_fusion.1 = f32[16,12288]{0,1:T(8,128)} fusion(s32[1024]{0:T(1024)S(1)} %bitcast.77, f32[1024,16]{1,0:T(8,128)} %copy.51, f32[]{:T(128)} %constant.15.clone.1), kind=kCustom, calls=%fused_computation.4 | custom fusion | flops 16384 | bytes 786944 | tf_op jit(solution)/shard_map/scatter-add | solution.py:152
  125.7 5.3 %copy.52 = f32[16,16,768]{2,1,0:T(8,128)} copy(f32[16,16,768]{0,2,1:T(8,128)} %bitcast.63) | data formatting | bytes 1572864 | tf_op jit(solution)/shard_map/reshape | solution.py:154
  131.0 1.5 %fusion.7 = f32[16,18,768]{2,1,0:T(8,128)S(1)} fusion(f32[16,2,768]{2,1,0:T(2,128)} %collective-permute-done.7, f32[16,16,768]{2,1,0:T(8,128)S(1)} %fusion.43, f32[16,2,768]{2,1,0:T(2,128)} %collective-permute-done.8, f32[16,1,768]{2,1,0:T(1,128)S(1)} %collective-permute-done.6, f32[16,16,768]{2,1,0:T(8,128)S(1)} %copy-done.1, ...), kind=kLoop, calls=%fused_computation.14 | loop fusion | flops 1548288 | bytes 2752512 | tf_op jit(solution)/shard_map/mul | solution.py:71
  133.1 0.6 fusion.19
  133.8 0.5 fusion.36
  134.4 2.0 %collective-permute-start.10 = (f32[16,2,768]{2,1,0:T(2,128)S(1)}, f32[16,2,768]{2,1,0:T(2,128)S(1)}, u32[]{:S(2)}, u32[]{:S(2)}) collective-permute-start(f32[16,2,768]{2,1,0:T(2,128)S(1)} %get-tuple-element.8), channel_id=1, source_target_pairs={{0,1},{1,2},{2,3},{3,4},{4,5},{5,6},{6,7},{7,8},{8,9},{9,10},{10,1... | collective-permute-start | bytes 294920 | tf_op jit(solution)/shard_map/ppermute | solution.py:15
  136.4 2.6 %collective-permute-done.9 = f32[16,2,768]{2,1,0:T(2,128)S(1)} collective-permute-done((f32[16,2,768]{2,1,0:T(2,128)S(1)}, f32[16,2,768]{2,1,0:T(2,128)S(1)}, u32[]{:S(2)}, u32[]{:S(2)}) %collective-permute-start.9) | collective-permute-done | bytes 98336 | tf_op jit(solution)/shard_map/ppermute | solution.py:18
  139.0 3.7 %collective-permute-done.10 = f32[16,2,768]{2,1,0:T(2,128)S(1)} collective-permute-done((f32[16,2,768]{2,1,0:T(2,128)S(1)}, f32[16,2,768]{2,1,0:T(2,128)S(1)}, u32[]{:S(2)}, u32[]{:S(2)}) %collective-permute-start.10) | collective-permute-done | bytes 98336 | tf_op jit(solution)/shard_map/ppermute | solution.py:15
  143.1 1.1 fusion.33
  (48 shorter events, 4.1 us)
Async XLA Ops:
  0.0 28.4 %copy-start.1 = (f32[16,16,768]{2,1,0:T(8,128)S(1)}, f32[16,16,768]{2,1,0:T(8,128)}, u32[]{:S(2)}) copy-start(f32[16,16,768]{2,1,0:T(8,128)} %param.15) | copy-start | bytes 2359300
  0.0 13.8 %all-to-all-start = ((s32[1,8,128]{2,0,1:T(1,128)}), s32[1,8,128]{2,0,1:T(1,128)S(1)}, u32[]{:S(2)}, u32[]{:S(2)}) async-start(s32[1,8,128]{2,0,1:T(1,128)} %bitcast.75), calls=%async_computation | async-start | bytes 8192 | tf_op jit(solution)/shard_map/all_to_all | solution.py:132
  7.4 12.2 %collective-permute-start = (f32[16,16,768]{2,1,0:T(8,128)}, f32[16,16,768]{2,1,0:T(8,128)S(1)}, u32[]{:S(2)}, u32[]{:S(2)}) collective-permute-start(f32[16,16,768]{2,1,0:T(8,128)} %param.13), channel_id=1, source_target_pairs={{24,0},{0,8},{8,16},{16,24},{25,1},{1,9},{9,17},{17,25},{26,2},{2,... | collective-permute-start | bytes 2359304 | tf_op jit(solution)/shard_map/ppermute | solution.py:26
  9.2 15.8 %collective-permute-start.1 = (f32[16,1,768]{2,1,0:T(1,128)S(1)}, f32[16,1,768]{2,1,0:T(1,128)S(1)}, u32[]{:S(2)}, u32[]{:S(2)}) collective-permute-start(f32[16,1,768]{2,1,0:T(1,128)S(1)} %get-tuple-element.13), channel_id=1, source_target_pairs={{0,1},{1,2},{2,3},{3,4},{4,5},{5,6},{6,7},{7,8},{8,9},{9,10},{10,1... | collective-permute-start | bytes 147464 | tf_op jit(solution)/shard_map/ppermute | solution.py:15
  13.8 39.1 %all-to-all-start.2 = ((f32[1,8,128]{2,0,1:T(1,128)}), f32[1,8,128]{2,0,1:T(1,128)S(1)}, u32[]{:S(2)}, u32[]{:S(2)}) async-start(f32[1,8,128]{2,0,1:T(1,128)} %compare_select_fusion.1), calls=%async_computation.2 | async-start | bytes 8192 | tf_op jit(solution)/shard_map/all_to_all | solution.py:128
  19.6 8.7 %collective-permute-start.3 = (f32[16,2,768]{2,1,0:T(2,128)S(1)}, f32[16,2,768]{2,1,0:T(2,128)S(1)}, u32[]{:S(2)}, u32[]{:S(2)}) collective-permute-start(f32[16,2,768]{2,1,0:T(2,128)S(1)} %get-tuple-element.27), channel_id=1, source_target_pairs={{0,1},{1,2},{2,3},{3,4},{4,5},{5,6},{6,7},{7,8},{8,9},{9,10},{10,1... | collective-permute-start | bytes 294920 | tf_op jit(solution)/shard_map/ppermute | solution.py:15
  21.2 7.2 %collective-permute-start.2 = (f32[16,2,768]{2,1,0:T(2,128)S(1)}, f32[16,2,768]{2,1,0:T(2,128)S(1)}, u32[]{:S(2)}, u32[]{:S(2)}) collective-permute-start(f32[16,2,768]{2,1,0:T(2,128)S(1)} %get-tuple-element.26), channel_id=1, source_target_pairs={{1,0},{2,1},{3,2},{4,3},{5,4},{6,5},{7,6},{8,7},{9,8},{10,9},{11,1... | collective-permute-start | bytes 294920 | tf_op jit(solution)/shard_map/ppermute | solution.py:18
  29.0 1.1 copy-start
  30.9 1.1 copy-start.2
  33.0 16.1 %collective-permute-start.5 = (f32[16,2,768]{2,1,0:T(2,128)}, f32[16,2,768]{2,1,0:T(2,128)S(1)}, u32[]{:S(2)}, u32[]{:S(2)}) collective-permute-start(f32[16,2,768]{2,1,0:T(2,128)} %get-tuple-element.23), channel_id=1, source_target_pairs={{0,1},{1,2},{2,3},{3,4},{4,5},{5,6},{6,7},{7,8},{8,9},{9,10},{10,1... | collective-permute-start | bytes 294920 | tf_op jit(solution)/shard_map/ppermute | solution.py:15
  33.0 16.1 %collective-permute-start.4 = (f32[16,2,768]{2,1,0:T(2,128)}, f32[16,2,768]{2,1,0:T(2,128)}, u32[]{:S(2)}, u32[]{:S(2)}) collective-permute-start(f32[16,2,768]{2,1,0:T(2,128)} %get-tuple-element.22), channel_id=1, source_target_pairs={{1,0},{2,1},{3,2},{4,3},{5,4},{6,5},{7,6},{8,7},{9,8},{10,9},{11,1... | collective-permute-start | bytes 294920 | tf_op jit(solution)/shard_map/ppermute | solution.py:18
  52.9 17.3 %all-to-all-start.4 = ((f32[1,8,128]{2,0,1:T(1,128)}), f32[1,8,128]{2,0,1:T(1,128)S(1)}, u32[]{:S(2)}, u32[]{:S(2)}) async-start(f32[1,8,128]{2,0,1:T(1,128)} %bitcast.22), calls=%async_computation.4 | async-start | bytes 8192 | tf_op jit(solution)/shard_map/all_to_all | solution.py:127
  70.3 12.8 %all-to-all-start.3 = ((f32[1,8,16,128]{3,2,0,1:T(8,128)}), f32[1,8,16,128]{3,2,0,1:T(8,128)S(1)}, u32[]{:S(2)}, u32[]{:S(2)}) async-start(f32[1,8,16,128]{3,2,0,1:T(8,128)} %bitcast.19), calls=%async_computation.3 | async-start | bytes 131072 | tf_op jit(solution)/shard_map/all_to_all | solution.py:129
  83.1 9.7 %all-to-all-start.1 = ((s32[1,8,128]{2,0,1:T(1,128)}), s32[1,8,128]{2,0,1:T(1,128)S(1)}, u32[]{:S(2)}, u32[]{:S(2)}) async-start(s32[1,8,128]{2,0,1:T(1,128)} %bitcast.7), calls=%async_computation.1 | async-start | bytes 8192 | tf_op jit(solution)/shard_map/all_to_all | solution.py:133
  109.9 21.1 %collective-permute-start.7 = (f32[16,2,768]{2,1,0:T(2,128)}, f32[16,2,768]{2,1,0:T(2,128)}, u32[]{:S(2)}, u32[]{:S(2)}) collective-permute-start(f32[16,2,768]{2,1,0:T(2,128)} %get-tuple-element.15), channel_id=1, source_target_pairs={{1,0},{2,1},{3,2},{4,3},{5,4},{6,5},{7,6},{8,7},{9,8},{10,9},{11,1... | collective-permute-start | bytes 294920 | tf_op jit(solution)/shard_map/ppermute | solution.py:18
  109.9 21.1 %collective-permute-start.8 = (f32[16,2,768]{2,1,0:T(2,128)}, f32[16,2,768]{2,1,0:T(2,128)}, u32[]{:S(2)}, u32[]{:S(2)}) collective-permute-start(f32[16,2,768]{2,1,0:T(2,128)} %get-tuple-element.14), channel_id=1, source_target_pairs={{0,1},{1,2},{2,3},{3,4},{4,5},{5,6},{6,7},{7,8},{8,9},{9,10},{10,1... | collective-permute-start | bytes 294920 | tf_op jit(solution)/shard_map/ppermute | solution.py:15
  111.9 19.1 %collective-permute-start.6 = (f32[16,1,768]{2,1,0:T(1,128)}, f32[16,1,768]{2,1,0:T(1,128)S(1)}, u32[]{:S(2)}, u32[]{:S(2)}) collective-permute-start(f32[16,1,768]{2,1,0:T(1,128)} %get-tuple-element.12), channel_id=1, source_target_pairs={{1,0},{2,1},{3,2},{4,3},{5,4},{6,5},{7,6},{8,7},{9,8},{10,9},{11,1... | collective-permute-start | bytes 147464 | tf_op jit(solution)/shard_map/ppermute | solution.py:18
  131.0 1.5 %copy-start.3 = (f32[16,16,768]{2,1,0:T(8,128)S(1)}, f32[16,16,768]{2,1,0:T(8,128)}, u32[]{:S(2)}) copy-start(f32[16,16,768]{2,1,0:T(8,128)} %copy.52) | copy-start | bytes 2359300
  134.3 4.7 %collective-permute-start.9 = (f32[16,2,768]{2,1,0:T(2,128)S(1)}, f32[16,2,768]{2,1,0:T(2,128)S(1)}, u32[]{:S(2)}, u32[]{:S(2)}) collective-permute-start(f32[16,2,768]{2,1,0:T(2,128)S(1)} %get-tuple-element.9), channel_id=1, source_target_pairs={{1,0},{2,1},{3,2},{4,3},{5,4},{6,5},{7,6},{8,7},{9,8},{10,9},{11,1... | collective-permute-start | bytes 294920 | tf_op jit(solution)/shard_map/ppermute | solution.py:18
  134.4 8.3 %collective-permute-start.10 = (f32[16,2,768]{2,1,0:T(2,128)S(1)}, f32[16,2,768]{2,1,0:T(2,128)S(1)}, u32[]{:S(2)}, u32[]{:S(2)}) collective-permute-start(f32[16,2,768]{2,1,0:T(2,128)S(1)} %get-tuple-element.8), channel_id=1, source_target_pairs={{0,1},{1,2},{2,3},{3,4},{4,5},{5,6},{6,7},{7,8},{8,9},{9,10},{10,1... | collective-permute-start | bytes 294920 | tf_op jit(solution)/shard_map/ppermute | solution.py:15
where the time goes:
time: 145 us; the launch traced here: 144 us
  starting transfers between devices  45.2 us (31%)
  local copies, waits for them, and re-layouts  41.3 us (28%)
  other arithmetic  37.4 us (26%)
  waiting for transfers between devices  20.1 us (14%)
    scatter-add x2, other arithmetic, on_device(): jnp.zeros((levels, width_x * width_y), jnp.float32).at[:, cell_index]  18.4 us
    gather x2, local copies, waits for them, and re-layouts, on_device(): jnp.take(flattened, cell_index, axis=1)  13.6 us
    ppermute x5, starting transfers between devices, with_halo(): lax.ppermute(lax.slice_in_dim(block, 0, width, axis=dim), axis, backward)  12.6 us
    reshape x2, local copies, waits for them, and re-layouts, on_device(): forcings.append(forcing.reshape(levels, width_x, width_y))  9.79 us
    sub x2, local copies, waits for them, and re-layouts, vertical_mix(): field + jnp.concatenate([fluxes, zero_row], axis=0)  8.8 us
    ppermute x5, starting transfers between devices, with_halo(): lax.ppermute(lax.slice_in_dim(block, block.shape[dim] - width, None, axis...  7.6 us
    all_to_all x1, starting transfers between devices, on_device(): lax.all_to_all(snd_column, 'tile', split_axis=1, concat_axis=0, tiled=True)  7.41 us
    ppermute x5, waiting for transfers between devices, with_halo(): lax.ppermute(lax.slice_in_dim(block, block.shape[dim] - width, None, axis...  7 us
  transfers between devices with their start and end apart: 16, of which 7 were waited for; matrix products, arithmetic and copies ran while one was open for 38% of the time, Pallas kernels for 0%

commit v1 on v0

--- a/solution.py
+++ b/solution.py
@@ -4,6 +4,12 @@
 from jax.sharding import PartitionSpec as P
 
 STEPS = 2
+
+
+def swap_blocks(block, name, split, join):
+    parts = jnp.split(block, lax.axis_size(name), axis=split)
+    arrived = lax.all_to_all(jnp.stack(parts), name, 0, 0)
+    return jnp.concatenate(arrived, axis=join)
 
 
 def with_halo(block, sides, width):
@@ -126,7 +132,7 @@
     values, weights, kernels = (
         lax.all_to_all(snd_value, "tile", split_axis=1, concat_axis=0, tiled=True),
         lax.all_to_all(weight, "tile", split_axis=1, concat_axis=0, tiled=True),
-        lax.all_to_all(snd_kernel, "tile", split_axis=1, concat_axis=0, tiled=True),
+        swap_blocks(snd_kernel, "tile", 1, 0),
     )
     columns, step_ids = (
         lax.all_to_all(snd_column, "tile", split_axis=1, concat_axis=0, tiled=True),

time: 145 us -> 155 us (1.069)
  local copies, waits for them, and re-layouts: 41.3 us -> 51.6 us
    unnamed x10 -> x17, local copies, waits for them, and re-layouts: 3 us -> 12 us
  transfers between devices with their start and end apart: 16 -> 16, of which waited for: 7 -> 5; matrix products, arithmetic and copies ran while one was open for 38% -> 43% of each run, Pallas kernels for 0% -> 0%
where the time goes in v1:
time: 155 us; the launch traced here: 154 us
  local copies, waits for them, and re-layouts  51.6 us (33%)
  starting transfers between devices  45.4 us (29%)
  other arithmetic  37.4 us (24%)
  waiting for transfers between devices  19.1 us (12%)
    scatter-add x2, other arithmetic, on_device(): jnp.zeros((levels, width_x * width_y), jnp.float32).at[:, cell_index]  18.4 us
    gather x2, local copies, waits for them, and re-layouts, on_device(): jnp.take(flattened, cell_index, axis=1)  13.6 us
    unnamed x17, local copies, waits for them, and re-layouts  12 us
    ppermute x5, starting transfers between devices, with_halo(): lax.ppermute(lax.slice_in_dim(block, 0, width, axis=dim), axis, backward)  11.8 us
    reshape x2, local copies, waits for them, and re-layouts, on_device(): forcings.append(forcing.reshape(levels, width_x, width_y))  9.79 us
    sub x2, local copies, waits for them, and re-layouts, vertical_mix(): field + jnp.concatenate([fluxes, zero_row], axis=0)  8.8 us
    ppermute x5, starting transfers between devices, with_halo(): lax.ppermute(lax.slice_in_dim(block, block.shape[dim] - width, None, axis...  8.37 us
    all_to_all x1, starting transfers between devices, on_device(): lax.all_to_all(snd_column, 'tile', split_axis=1, concat_axis=0, tiled=True)  7.41 us
  transfers between devices with their start and end apart: 16, of which 5 were waited for; matrix products, arithmetic and copies ran while one was open for 43% of the time, Pallas kernels for 0%

profile of v1, /device:TPU:0, one launch (start us, length us, event | category | flops | bytes accessed | tf_op | source)
XLA Modules:
  0.0 153.8 jit_solution(2586987029472524530)
XLA Ops:
  0.0 7.4 %all-to-all-start = ((s32[1,8,128]{2,0,1:T(1,128)}), s32[1,8,128]{2,0,1:T(1,128)S(1)}, u32[]{:S(2)}, u32[]{:S(2)}) async-start(s32[1,8,128]{2,0,1:T(1,128)} %bitcast.90), calls=%async_computation | async-start | bytes 8192 | tf_op jit(solution)/shard_map/all_to_all | solution.py:138
  7.4 1.8 %fusion.56 = (f32[16,1,768]{2,1,0:T(1,128)}, f32[16,1,768]{2,1,0:T(1,128)S(1)}) fusion(f32[16,16,768]{2,1,0:T(8,128)} %param.15), kind=kLoop, calls=%fused_computation.134 | loop fusion | bytes 196608 | tf_op jit(solution)/shard_map/slice | solution.py:24
  9.2 2.0 %collective-permute-start.1 = (f32[16,1,768]{2,1,0:T(1,128)S(1)}, f32[16,1,768]{2,1,0:T(1,128)S(1)}, u32[]{:S(2)}, u32[]{:S(2)}) collective-permute-start(f32[16,1,768]{2,1,0:T(1,128)S(1)} %get-tuple-element.13), channel_id=1, source_target_pairs={{0,1},{1,2},{2,3},{3,4},{4,5},{5,6},{6,7},{7,8},{8,9},{9,10},{10,1... | collective-permute-start | bytes 147464 | tf_op jit(solution)/shard_map/ppermute | solution.py:21
  11.2 1.3 constant_dynamic-update-slice_fusion.7
  12.5 1.3 constant_dynamic-update-slice_fusion.6
  13.8 1.3 constant_dynamic-update-slice_fusion.5
  15.1 1.3 constant_dynamic-update-slice_fusion.4
  16.4 1.3 constant_dynamic-update-slice_fusion.3
  17.7 1.3 constant_dynamic-update-slice_fusion.2
  19.0 1.3 constant_dynamic-update-slice_fusion.1
  20.3 1.3 constant_dynamic-update-slice_fusion
  21.6 1.1 fusion.58
  22.6 1.4 compare_select_fusion.1
  24.0 5.2 %all-to-all-start.2 = ((f32[1,8,128]{2,0,1:T(1,128)}), f32[1,8,128]{2,0,1:T(1,128)S(1)}, u32[]{:S(2)}, u32[]{:S(2)}) async-start(f32[1,8,128]{2,0,1:T(1,128)} %compare_select_fusion.1), calls=%async_computation.2 | async-start | bytes 8192 | tf_op jit(solution)/shard_map/all_to_all | solution.py:134
  29.3 2.1 %collective-permute-start.3 = (f32[16,2,768]{2,1,0:T(2,128)S(1)}, f32[16,2,768]{2,1,0:T(2,128)S(1)}, u32[]{:S(2)}, u32[]{:S(2)}) collective-permute-start(f32[16,2,768]{2,1,0:T(2,128)S(1)} %get-tuple-element.27), channel_id=1, source_target_pairs={{0,1},{1,2},{2,3},{3,4},{4,5},{5,6},{6,7},{7,8},{8,9},{9,10},{10,1... | collective-permute-start | bytes 294920 | tf_op jit(solution)/shard_map/ppermute | solution.py:21
  31.4 3.3 %collective-permute-start.2 = (f32[16,2,768]{2,1,0:T(2,128)S(1)}, f32[16,2,768]{2,1,0:T(2,128)S(1)}, u32[]{:S(2)}, u32[]{:S(2)}) collective-permute-start(f32[16,2,768]{2,1,0:T(2,128)S(1)} %get-tuple-element.26), channel_id=1, source_target_pairs={{1,0},{2,1},{3,2},{4,3},{5,4},{6,5},{7,6},{8,7},{9,8},{10,9},{11,1... | collective-permute-start | bytes 294920 | tf_op jit(solution)/shard_map/ppermute | solution.py:24
  34.7 3.4 %collective-permute-done.3 = f32[16,2,768]{2,1,0:T(2,128)S(1)} collective-permute-done((f32[16,2,768]{2,1,0:T(2,128)S(1)}, f32[16,2,768]{2,1,0:T(2,128)S(1)}, u32[]{:S(2)}, u32[]{:S(2)}) %collective-permute-start.3) | collective-permute-done | bytes 98336 | tf_op jit(solution)/shard_map/ppermute | solution.py:21
  39.0 0.9 copy-done
  39.8 0.8 fusion.29
  43.0 5.1 %collective-permute-start.4 = (f32[16,2,768]{2,1,0:T(2,128)}, f32[16,2,768]{2,1,0:T(2,128)}, u32[]{:S(2)}, u32[]{:S(2)}) collective-permute-start(f32[16,2,768]{2,1,0:T(2,128)} %get-tuple-element.22), channel_id=1, source_target_pairs={{1,0},{2,1},{3,2},{4,3},{5,4},{6,5},{7,6},{8,7},{9,8},{10,9},{11,1... | collective-permute-start | bytes 294920 | tf_op jit(solution)/shard_map/ppermute | solution.py:24
  48.1 3.9 %copy.47 = f32[16,16,768]{0,2,1:T(8,128)} copy(f32[16,16,768]{2,1,0:T(8,128)S(1)} %pad_subtract_fusion.3) | data formatting | bytes 1572864 | tf_op jit(solution)/shard_map/sub | solution.py:93
  52.0 6.8 %gather_fusion.1 = f32[1024,16]{1,0:T(8,128)} fusion(f32[16,12288]{0,1:T(8,128)} %bitcast.81, s32[1024]{0:T(1024)S(1)} %fusion.53), kind=kCustom, calls=%fused_computation.1.clone | custom fusion | bytes 135168 | tf_op jit(solution)/shard_map/jit(_take)/gather | solution.py:149
  58.8 1.5 fusion.10
  60.6 0.8 fusion.24
  61.7 0.9 fusion.47
  62.7 3.3 %all-to-all-start.4 = ((f32[1,8,128]{2,0,1:T(1,128)}), f32[1,8,128]{2,0,1:T(1,128)S(1)}, u32[]{:S(2)}, u32[]{:S(2)}) async-start(f32[1,8,128]{2,0,1:T(1,128)} %bitcast.29), calls=%async_computation.4 | async-start | bytes 8192 | tf_op jit(solution)/shard_map/all_to_all | solution.py:133
  66.0 2.3 %pad_subtract_fusion.2 = f32[16,16,768]{2,1,0:T(8,128)} fusion(f32[15,16,768]{2,1,0:T(8,128)} %fusion.47, f32[16,16,768]{2,1,0:T(8,128)S(1)} %slice_subtract_fusion.4), kind=kLoop, calls=%fused_computation.95 | loop fusion | flops 393216 | bytes 2310144 | tf_op jit(solution)/shard_map/sub | solution.py:93
  68.4 4.8 %copy.41 = f32[16,16,768]{0,2,1:T(8,128)} copy(f32[16,16,768]{2,1,0:T(8,128)} %pad_subtract_fusion.2) | data formatting | bytes 1572864 | tf_op jit(solution)/shard_map/sub | solution.py:93
  73.2 6.8 %gather_fusion = f32[1024,16]{1,0:T(8,128)} fusion(f32[16,12288]{0,1:T(8,128)} %bitcast.80, s32[1024]{0:T(1024)S(1)} %fusion.53), kind=kCustom, calls=%fused_computation.clone | custom fusion | bytes 135168 | tf_op jit(solution)/shard_map/jit(_take)/gather | solution.py:149
  80.0 5.9 %all-to-all-start.3 = ((f32[8,1,1,16,128]{4,3,2,1,0:T(8,128)}), f32[8,1,1,16,128]{4,3,2,1,0:T(8,128)S(1)}, u32[]{:S(2)}, u32[]{:S(2)}) async-start(f32[8,1,1,16,128]{4,3,2,1,0:T(8,128)} %constant_dynamic-update-slice_fusion), calls=%async_computation.3 | async-start | bytes 131072 | tf_op jit(solution)/shard_map/all_to_all | solution.py:11
  86.0 2.2 %broadcast_select_fusion = (f32[1024,16]{1,0:T(8,128)S(1)}, f32[1024,16]{1,0:T(8,128)}) fusion(f32[1024,16]{1,0:T(8,128)} %gather_fusion.1, pred[1024]{0:T(1024)(128)(4,1)S(1)} %compare_and_fusion, f32[1024,16]{1,0:T(8,128)} %gather_fusion), kind=kLoop, calls=%fused_computation.105 | loop fusion | flops 32768 | bytes 263168 | tf_op jit(solution)/shard_map/jit(_take)/select_n | solution.py:149
  88.1 1.2 copy.56
  89.5 3.3 %all-to-all-done.3 = f32[8,1,1,16,128]{4,3,2,1,0:T(8,128)S(1)} async-done(((f32[8,1,1,16,128]{4,3,2,1,0:T(8,128)}), f32[8,1,1,16,128]{4,3,2,1,0:T(8,128)S(1)}, u32[]{:S(2)}, u32[]{:S(2)}) %all-to-all-start.3) | async-done | bytes 65568 | tf_op jit(solution)/shard_map/all_to_all | solution.py:11
  92.9 3.3 %all-to-all-start.1 = ((s32[1,8,128]{2,0,1:T(1,128)}), s32[1,8,128]{2,0,1:T(1,128)S(1)}, u32[]{:S(2)}, u32[]{:S(2)}) async-start(s32[1,8,128]{2,0,1:T(1,128)} %bitcast.7), calls=%async_computation.1 | async-start | bytes 8192 | tf_op jit(solution)/shard_map/all_to_all | solution.py:139
  96.2 6.3 %all-to-all-done.1 = s32[1,8,128]{2,0,1:T(1,128)S(1)} async-done(((s32[1,8,128]{2,0,1:T(1,128)}), s32[1,8,128]{2,0,1:T(1,128)S(1)}, u32[]{:S(2)}, u32[]{:S(2)}) %all-to-all-start.1) | async-done | bytes 4128 | tf_op jit(solution)/shard_map/all_to_all | solution.py:139
  102.8 9.0 %scatter_custom_fusion = f32[16,12288]{0,1:T(8,128)} fusion(s32[1024]{0:T(1024)S(1)} %bitcast.91, f32[1024,16]{1,0:T(8,128)S(1)} %copy.44, f32[]{:T(128)} %constant.15.clone.1), kind=kCustom, calls=%fused_computation.6 | custom fusion | flops 16384 | bytes 786436 | tf_op jit(solution)/shard_map/scatter-add | solution.py:158
  111.8 4.5 %copy.45 = f32[16,16,768]{2,1,0:T(8,128)S(1)} copy(f32[16,16,768]{0,2,1:T(8,128)} %bitcast.79) | data formatting | bytes 1572864 | tf_op jit(solution)/shard_map/reshape | solution.py:160
  116.3 1.2 add.114
  119.7 2.0 %collective-permute-start.8 = (f32[16,2,768]{2,1,0:T(2,128)}, f32[16,2,768]{2,1,0:T(2,128)}, u32[]{:S(2)}, u32[]{:S(2)}) collective-permute-start(f32[16,2,768]{2,1,0:T(2,128)} %get-tuple-element.14), channel_id=1, source_target_pairs={{0,1},{1,2},{2,3},{3,4},{4,5},{5,6},{6,7},{7,8},{8,9},{9,10},{10,1... | collective-permute-start | bytes 294920 | tf_op jit(solution)/shard_map/ppermute | solution.py:21
  121.7 3.3 %collective-permute-start.6 = (f32[16,1,768]{2,1,0:T(1,128)}, f32[16,1,768]{2,1,0:T(1,128)S(1)}, u32[]{:S(2)}, u32[]{:S(2)}) collective-permute-start(f32[16,1,768]{2,1,0:T(1,128)} %get-tuple-element.12), channel_id=1, source_target_pairs={{1,0},{2,1},{3,2},{4,3},{5,4},{6,5},{7,6},{8,7},{9,8},{10,9},{11,1... | collective-permute-start | bytes 147464 | tf_op jit(solution)/shard_map/ppermute | solution.py:24
  125.0 1.0 copy.49
  126.0 9.4 %scatter_custom_fusion.1 = f32[16,12288]{0,1:T(8,128)} fusion(s32[1024]{0:T(1024)S(1)} %bitcast.92, f32[1024,16]{1,0:T(8,128)} %copy.49, f32[]{:T(128)} %constant.15.clone.1), kind=kCustom, calls=%fused_computation.4 | custom fusion | flops 16384 | bytes 786944 | tf_op jit(solution)/shard_map/scatter-add | solution.py:158
  135.4 5.3 %copy.50 = f32[16,16,768]{2,1,0:T(8,128)} copy(f32[16,16,768]{0,2,1:T(8,128)} %bitcast.78) | data formatting | bytes 1572864 | tf_op jit(solution)/shard_map/reshape | solution.py:160
  140.8 1.5 fusion.7
  144.2 2.0 %collective-permute-start.10 = (f32[16,2,768]{2,1,0:T(2,128)S(1)}, f32[16,2,768]{2,1,0:T(2,128)S(1)}, u32[]{:S(2)}, u32[]{:S(2)}) collective-permute-start(f32[16,2,768]{2,1,0:T(2,128)S(1)} %get-tuple-element.8), channel_id=1, source_target_pairs={{0,1},{1,2},{2,3},{3,4},{4,5},{5,6},{6,7},{7,8},{8,9},{9,10},{10,1... | collective-permute-start | bytes 294920 | tf_op jit(solution)/shard_map/ppermute | solution.py:21
  146.2 2.6 %collective-permute-done.9 = f32[16,2,768]{2,1,0:T(2,128)S(1)} collective-permute-done((f32[16,2,768]{2,1,0:T(2,128)S(1)}, f32[16,2,768]{2,1,0:T(2,128)S(1)}, u32[]{:S(2)}, u32[]{:S(2)}) %collective-permute-start.9) | collective-permute-done | bytes 98336 | tf_op jit(solution)/shard_map/ppermute | solution.py:24
  148.8 3.5 %collective-permute-done.10 = f32[16,2,768]{2,1,0:T(2,128)S(1)} collective-permute-done((f32[16,2,768]{2,1,0:T(2,128)S(1)}, f32[16,2,768]{2,1,0:T(2,128)S(1)}, u32[]{:S(2)}, u32[]{:S(2)}) %collective-permute-start.10) | collective-permute-done | bytes 98336 | tf_op jit(solution)/shard_map/ppermute | solution.py:21
  152.7 1.1 fusion.33
  (56 shorter events, 8.7 us)
Async XLA Ops:
  0.0 38.1 %copy-start.1 = (f32[16,16,768]{2,1,0:T(8,128)S(1)}, f32[16,16,768]{2,1,0:T(8,128)}, u32[]{:S(2)}) copy-start(f32[16,16,768]{2,1,0:T(8,128)} %param.15) | copy-start | bytes 2359300
  0.0 24.0 %all-to-all-start = ((s32[1,8,128]{2,0,1:T(1,128)}), s32[1,8,128]{2,0,1:T(1,128)S(1)}, u32[]{:S(2)}, u32[]{:S(2)}) async-start(s32[1,8,128]{2,0,1:T(1,128)} %bitcast.90), calls=%async_computation | async-start | bytes 8192 | tf_op jit(solution)/shard_map/all_to_all | solution.py:138
  7.4 21.8 %collective-permute-start = (f32[16,16,768]{2,1,0:T(8,128)}, f32[16,16,768]{2,1,0:T(8,128)S(1)}, u32[]{:S(2)}, u32[]{:S(2)}) collective-permute-start(f32[16,16,768]{2,1,0:T(8,128)} %param.13), channel_id=1, source_target_pairs={{24,0},{0,8},{8,16},{16,24},{25,1},{1,9},{9,17},{17,25},{26,2},{2,... | collective-permute-start | bytes 2359304 | tf_op jit(solution)/shard_map/ppermute | solution.py:32
  9.2 25.5 %collective-permute-start.1 = (f32[16,1,768]{2,1,0:T(1,128)S(1)}, f32[16,1,768]{2,1,0:T(1,128)S(1)}, u32[]{:S(2)}, u32[]{:S(2)}) collective-permute-start(f32[16,1,768]{2,1,0:T(1,128)S(1)} %get-tuple-element.13), channel_id=1, source_target_pairs={{0,1},{1,2},{2,3},{3,4},{4,5},{5,6},{6,7},{7,8},{8,9},{9,10},{10,1... | collective-permute-start | bytes 147464 | tf_op jit(solution)/shard_map/ppermute | solution.py:21
  24.0 38.7 %all-to-all-start.2 = ((f32[1,8,128]{2,0,1:T(1,128)}), f32[1,8,128]{2,0,1:T(1,128)S(1)}, u32[]{:S(2)}, u32[]{:S(2)}) async-start(f32[1,8,128]{2,0,1:T(1,128)} %compare_select_fusion.1), calls=%async_computation.2 | async-start | bytes 8192 | tf_op jit(solution)/shard_map/all_to_all | solution.py:134
  29.3 8.8 %collective-permute-start.3 = (f32[16,2,768]{2,1,0:T(2,128)S(1)}, f32[16,2,768]{2,1,0:T(2,128)S(1)}, u32[]{:S(2)}, u32[]{:S(2)}) collective-permute-start(f32[16,2,768]{2,1,0:T(2,128)S(1)} %get-tuple-element.27), channel_id=1, source_target_pairs={{0,1},{1,2},{2,3},{3,4},{4,5},{5,6},{6,7},{7,8},{8,9},{9,10},{10,1... | collective-permute-start | bytes 294920 | tf_op jit(solution)/shard_map/ppermute | solution.py:21
  31.4 6.7 %collective-permute-start.2 = (f32[16,2,768]{2,1,0:T(2,128)S(1)}, f32[16,2,768]{2,1,0:T(2,128)S(1)}, u32[]{:S(2)}, u32[]{:S(2)}) collective-permute-start(f32[16,2,768]{2,1,0:T(2,128)S(1)} %get-tuple-element.26), channel_id=1, source_target_pairs={{1,0},{2,1},{3,2},{4,3},{5,4},{6,5},{7,6},{8,7},{9,8},{10,9},{11,1... | collective-permute-start | bytes 294920 | tf_op jit(solution)/shard_map/ppermute | solution.py:24
  38.7 1.1 copy-start
  40.7 1.1 copy-start.2
  42.7 16.1 %collective-permute-start.5 = (f32[16,2,768]{2,1,0:T(2,128)}, f32[16,2,768]{2,1,0:T(2,128)S(1)}, u32[]{:S(2)}, u32[]{:S(2)}) collective-permute-start(f32[16,2,768]{2,1,0:T(2,128)} %get-tuple-element.23), channel_id=1, source_target_pairs={{0,1},{1,2},{2,3},{3,4},{4,5},{5,6},{6,7},{7,8},{8,9},{9,10},{10,1... | collective-permute-start | bytes 294920 | tf_op jit(solution)/shard_map/ppermute | solution.py:21
  43.0 15.9 %collective-permute-start.4 = (f32[16,2,768]{2,1,0:T(2,128)}, f32[16,2,768]{2,1,0:T(2,128)}, u32[]{:S(2)}, u32[]{:S(2)}) collective-permute-start(f32[16,2,768]{2,1,0:T(2,128)} %get-tuple-element.22), channel_id=1, source_target_pairs={{1,0},{2,1},{3,2},{4,3},{5,4},{6,5},{7,6},{8,7},{9,8},{10,9},{11,1... | collective-permute-start | bytes 294920 | tf_op jit(solution)/shard_map/ppermute | solution.py:24
  62.7 17.3 %all-to-all-start.4 = ((f32[1,8,128]{2,0,1:T(1,128)}), f32[1,8,128]{2,0,1:T(1,128)S(1)}, u32[]{:S(2)}, u32[]{:S(2)}) async-start(f32[1,8,128]{2,0,1:T(1,128)} %bitcast.29), calls=%async_computation.4 | async-start | bytes 8192 | tf_op jit(solution)/shard_map/all_to_all | solution.py:133
  80.0 12.8 %all-to-all-start.3 = ((f32[8,1,1,16,128]{4,3,2,1,0:T(8,128)}), f32[8,1,1,16,128]{4,3,2,1,0:T(8,128)S(1)}, u32[]{:S(2)}, u32[]{:S(2)}) async-start(f32[8,1,1,16,128]{4,3,2,1,0:T(8,128)} %constant_dynamic-update-slice_fusion), calls=%async_computation.3 | async-start | bytes 131072 | tf_op jit(solution)/shard_map/all_to_all | solution.py:11
  92.9 9.7 %all-to-all-start.1 = ((s32[1,8,128]{2,0,1:T(1,128)}), s32[1,8,128]{2,0,1:T(1,128)S(1)}, u32[]{:S(2)}, u32[]{:S(2)}) async-start(s32[1,8,128]{2,0,1:T(1,128)} %bitcast.7), calls=%async_computation.1 | async-start | bytes 8192 | tf_op jit(solution)/shard_map/all_to_all | solution.py:139
  119.7 21.1 %collective-permute-start.7 = (f32[16,2,768]{2,1,0:T(2,128)}, f32[16,2,768]{2,1,0:T(2,128)}, u32[]{:S(2)}, u32[]{:S(2)}) collective-permute-start(f32[16,2,768]{2,1,0:T(2,128)} %get-tuple-element.15), channel_id=1, source_target_pairs={{1,0},{2,1},{3,2},{4,3},{5,4},{6,5},{7,6},{8,7},{9,8},{10,9},{11,1... | collective-permute-start | bytes 294920 | tf_op jit(solution)/shard_map/ppermute | solution.py:24
  119.7 21.1 %collective-permute-start.8 = (f32[16,2,768]{2,1,0:T(2,128)}, f32[16,2,768]{2,1,0:T(2,128)}, u32[]{:S(2)}, u32[]{:S(2)}) collective-permute-start(f32[16,2,768]{2,1,0:T(2,128)} %get-tuple-element.14), channel_id=1, source_target_pairs={{0,1},{1,2},{2,3},{3,4},{4,5},{5,6},{6,7},{7,8},{8,9},{9,10},{10,1... | collective-permute-start | bytes 294920 | tf_op jit(solution)/shard_map/ppermute | solution.py:21
  121.7 19.1 %collective-permute-start.6 = (f32[16,1,768]{2,1,0:T(1,128)}, f32[16,1,768]{2,1,0:T(1,128)S(1)}, u32[]{:S(2)}, u32[]{:S(2)}) collective-permute-start(f32[16,1,768]{2,1,0:T(1,128)} %get-tuple-element.12), channel_id=1, source_target_pairs={{1,0},{2,1},{3,2},{4,3},{5,4},{6,5},{7,6},{8,7},{9,8},{10,9},{11,1... | collective-permute-start | bytes 147464 | tf_op jit(solution)/shard_map/ppermute | solution.py:24
  140.7 1.5 copy-start.3
  144.1 4.7 %collective-permute-start.9 = (f32[16,2,768]{2,1,0:T(2,128)S(1)}, f32[16,2,768]{2,1,0:T(2,128)S(1)}, u32[]{:S(2)}, u32[]{:S(2)}) collective-permute-start(f32[16,2,768]{2,1,0:T(2,128)S(1)} %get-tuple-element.9), channel_id=1, source_target_pairs={{1,0},{2,1},{3,2},{4,3},{5,4},{6,5},{7,6},{8,7},{9,8},{10,9},{11,1... | collective-permute-start | bytes 294920 | tf_op jit(solution)/shard_map/ppermute | solution.py:24
  144.2 8.1 %collective-permute-start.10 = (f32[16,2,768]{2,1,0:T(2,128)S(1)}, f32[16,2,768]{2,1,0:T(2,128)S(1)}, u32[]{:S(2)}, u32[]{:S(2)}) collective-permute-start(f32[16,2,768]{2,1,0:T(2,128)S(1)} %get-tuple-element.8), channel_id=1, source_target_pairs={{0,1},{1,2},{2,3},{3,4},{4,5},{5,6},{6,7},{7,8},{8,9},{9,10},{10,1... | collective-permute-start | bytes 294920 | tf_op jit(solution)/shard_map/ppermute | solution.py:21
